TPU v7x, 256 devices: a whole 4x4x8 slice. The times are simulated.
256 devices in a mesh: chain: 8 (over x, core), depth: 32 (over y, z).
Axes of the slice: x: 4, y: 4, z: 8, core: 2. Of those that a mesh axis runs over, the one named last changes fastest.
Arguments:
- model_field: float32 [2048, 2048], P(('chain', 'depth')), parts along dimension 0, may hold values from -4 to 4
- column_rate: float32 [16384], P('chain'), parts along dimension 0, may hold values from 0.2 to 20
- wavelets: float32 [128, 2048], P('chain'), parts along dimension 0, may hold values from -6 to 6
- source_depth: int32 [128], P('chain'), parts along dimension 0, may hold values from 0 to 255
- observed: float32 [2048, 16, 2048], P(('chain', 'depth')), parts along dimension 0, may hold values from -3 to 3
- basis: bfloat16 [2048, 256, 2048], P('chain', 'depth'), parts along dimension 0, may hold values from -0.03125 to 0.03125
- curvature: float32 [2048], P('chain'), parts along dimension 0, may hold values from 0.5 to 50
- noise_draw: float32 [2048, 2048], P(('chain', 'depth')), parts along dimension 0, may hold values from -6 to 6
Outputs:
- proposal: float32 [2048, 2048], P(('chain', 'depth')), parts along dimension 0
- log_gain: float32 [8], P('chain'), parts along dimension 0
There are 8 independent parts, one for each index of `chain`. A program takes and returns all parts, laid end to end along the dimension named above; each array names one. Nothing has to cross between parts.
All inputs are finite; a program needn't handle non-finite values.
Results may differ from a plain program's by a relative error of at most 0.0003.
The roundings to bfloat16 on the way count: a program that leaves them out, or rounds other values in their place, can miss the bound.
Values sent between devices are 32-bit elements; how exact they have to be, the bound alone decides.
A program may use at most 64 MiB of HBM per device.

v0:
```python
import jax
import jax.numpy as jnp
from jax import lax
from jax.sharding import Mesh
from jax.sharding import PartitionSpec as P

DEPTH = ("depth_0", "depth_1")
CHAIN_DEPTH = ("chain", "depth_0", "depth_1")


def filled_with(shard, identity):
    return jax.tree.map(
        lambda part, zero: jnp.zeros_like(part) + jnp.asarray(zero, part.dtype), shard, identity
    )


def prefix_by_axis(shard, axes, combine, identity, reverse):
    before = start = filled_with(shard, identity)
    subtotal = shard
    for axis in reversed(axes):
        count, position = (lax.axis_size(axis), lax.axis_index(axis))
        pieces = jax.tree.map(lambda part: lax.all_gather(part, axis), subtotal)
        inside, subtotal = (start, start)
        for k in reversed(range(count)) if reverse else range(count):
            passed = k > position if reverse else k < position
            subtotal = combine(subtotal, jax.tree.map(lambda part: part[k], pieces))
            inside = jax.tree.map(lambda new, old: jnp.where(passed, new, old), subtotal, inside)
        before = combine(inside, before)
    return before


def copy_for_each(shard, axis):
    count = lax.axis_size(axis)
    return lax.all_to_all(
        jnp.broadcast_to(shard[None], (count, *shard.shape)), axis, 0, 0, tiled=True
    )


def over_copies(shard, axis):
    return copy_for_each(shard, axis).sum(axis=0)


def compose(earlier, later):
    return (earlier[0] + later[0], jnp.exp(later[0])[None, :] * earlier[1] + later[1])


def enter_down(log_block, outgoing):
    identity = (jnp.zeros_like(log_block), jnp.zeros_like(outgoing))
    _, carry = prefix_by_axis((log_block, outgoing), DEPTH, compose, identity, False)
    return carry


def enter_up(log_block, outgoing):
    identity = (jnp.zeros_like(log_block), jnp.zeros_like(outgoing))
    _, carry = prefix_by_axis((log_block, outgoing), DEPTH, compose, identity, True)
    return carry


def march_down(model, column_rate, wavelets, source_depth, depth_count):
    coef = (column_rate / depth_count)[None, :] * jnp.exp(0.5 * model)
    decay = jnp.exp(-coef)
    running = jnp.cumsum(coef, axis=0)
    first = lax.axis_index(DEPTH) * model.shape[0]
    layers = first + jnp.arange(model.shape[0], dtype=jnp.int32)

    def advance(state, inputs):
        factor, layer = inputs
        inject = jnp.where((source_depth == layer)[:, None], wavelets, jnp.zeros_like(wavelets))
        state = factor[None, :] * state + inject
        return (state, state)

    start = jnp.zeros(wavelets.shape, jnp.float32)
    last, fields = lax.scan(advance, start, (decay, layers))
    carry = enter_down(-running[-1], last)
    fields = fields + jnp.exp(-running)[:, None, :] * carry[None]
    return (coef, decay, running, carry, fields)


def local(model_field, column_rate, wavelets, source_depth, observed, basis, curvature, noise_draw):
    depth_count = model_field.shape[0] * lax.axis_size(DEPTH)
    sources = wavelets.shape[0]
    coef, decay, running, carry, fields = march_down(
        model_field, column_rate, wavelets, source_depth, depth_count
    )
    resid = fields - observed
    energy_now = jnp.sum(resid * resid) / sources + 0.5 * jnp.sum(model_field * model_field)

    def retreat(state, inputs):
        factor, residual_layer = inputs
        adjoint = residual_layer + state
        return (factor[None, :] * adjoint, adjoint)

    upper, adjoints = lax.scan(
        retreat, jnp.zeros(resid.shape[1:], jnp.float32), (decay, resid), reverse=True
    )
    below = enter_up(-running[-1], upper)
    adjoints = adjoints + jnp.exp(running - running[-1:])[:, None, :] * below[None]
    previous = jnp.concatenate([carry[None], fields[:-1]], axis=0)
    gradient = model_field - coef * decay / sources * jnp.sum(adjoints * previous, axis=1)
    flat_basis = basis.reshape(basis.shape[0], -1)
    stacked = jnp.stack([gradient.reshape(-1), noise_draw.reshape(-1)]).astype(jnp.bfloat16)
    local_proj = lax.dot_general(
        stacked, flat_basis, (((1,), (1,)), ((), ())), preferred_element_type=jnp.float32
    )
    projected, energy_total = (over_copies(local_proj, DEPTH), over_copies(energy_now, DEPTH))
    damping = curvature / (1.0 + curvature)
    shrink = 1.0 - 1.0 / jnp.sqrt(1.0 + curvature)
    mixed = (damping * projected[0] - shrink * projected[1]).astype(jnp.bfloat16)
    correction = jnp.dot(mixed, flat_basis, preferred_element_type=jnp.float32).reshape(
        model_field.shape
    )
    proposal = model_field - gradient + noise_draw + correction
    fields_next = march_down(proposal, column_rate, wavelets, source_depth, depth_count)[4]
    resid_next = fields_next - observed
    energy_next = jnp.sum(resid_next * resid_next) / sources + 0.5 * jnp.sum(proposal * proposal)
    after = over_copies(energy_next, DEPTH)
    cells = depth_count * model_field.shape[1]
    log_gain = jnp.reshape((energy_total - after) / cells, (1,))
    return (proposal, log_gain)


def solution(mesh):
    split = Mesh(mesh.devices.reshape(mesh.shape["chain"], 4, 8), ("chain", "depth_0", "depth_1"))
    in_specs = (
        P(CHAIN_DEPTH, None),
        P("chain"),
        P("chain", None),
        P("chain"),
        P(CHAIN_DEPTH, None, None),
        P("chain", DEPTH, None),
        P("chain"),
        P(CHAIN_DEPTH, None),
    )
    out_specs = (P(CHAIN_DEPTH, None), P("chain"))
    return jax.shard_map(local, mesh=split, in_specs=in_specs, out_specs=out_specs, check_vma=False)
```

profile of v0, /device:TPU:2, one launch (start us, length us, event | category | flops | bytes accessed | tf_op | source)
XLA Modules:
  0.0 309.0 jit_solution(14377709018311472213)
XLA Ops:
  9.0 23.4 %while.43 = (s32[]{:T(128)}, f32[16,2048]{1,0:T(8,128)S(1)}, f32[8,16,2048]{2,1,0:T(8,128)S(1)}, f32[8,2048]{1,0:T(8,128)S(1)}, s32[8]{0:T(128)S(1)}, /*index=5*...) while((s32[]{:T(128)}, f32[16,2048]{1,0:T(8,128)S(1)}, f32[8,16,2048]{2,1,0:T(8,128)S(1)}, ...), condition=%wide.region_1.2_spmd.clone, body=%wide.region_0.0_spmd.clone.sunk | while | flops 131091 | bytes 549583 | solution.py:73
  9.6 1.3 broadcast_compare_fusion.4
  12.5 1.3 broadcast_compare_fusion.4
  15.5 1.3 broadcast_compare_fusion.4
  21.3 1.3 broadcast_compare_fusion.4
  24.2 1.3 broadcast_compare_fusion.4
  33.3 28.2 %all-gather.3 = f32[8,1,2048]{2,1,0:T(1,128)S(1)} all-gather(f32[1,1,2048]{2,1,0:T(1,128)S(1)} %get-tuple-element.329), channel_id=1, replica_groups=mesh['chain'=8,'depth_0'=4,'depth_1'=8] {'depth_1'}, dimensions={0}, use_global_device_ids=true | all-gather | bytes 73728 | tf_op jit(solution)/shard_map/all_gather | solution.py:22
  61.6 12.4 %all-gather.4 = f32[4,1,2048]{2,1,0:T(1,128)S(1)} all-gather(f32[1,1,2048]{2,1,0:T(1,128)S(1)} %get-tuple-element.337), channel_id=1, replica_groups=mesh['chain'=8,'depth_0'=4,'depth_1'=8] {'depth_0'}, dimensions={0}, use_global_device_ids=true | all-gather | bytes 40960 | tf_op jit(solution)/shard_map/all_gather | solution.py:22
  75.5 1.4 fusion.33
  76.9 12.8 %all_gather.56 = f32[4,16,2048]{2,1,0:T(8,128)S(1)} all-gather(f32[1,16,2048]{2,1,0:T(8,128)S(1)} %get-tuple-element.311), channel_id=1, replica_groups=mesh['chain'=8,'depth_0'=4,'depth_1'=8] {'depth_0'}, dimensions={0}, use_global_device_ids=true | all-gather | bytes 655360 | tf_op jit(solution)/shard_map/all_gather | solution.py:22
  89.7 1.4 fusion.32
  91.1 1.8 multiply_reduce_fusion.1
  94.8 16.3 %copy.23 = bf16[32,8,8,2048]{3,1,2,0:T(8,128)(2,1)} copy(bf16[32,8,8,2048]{3,2,1,0:T(8,128)(2,1)} %bitcast.503) | data formatting | bytes 16777216
  111.2 11.9 %all-gather.5 = f32[4,1,2048]{2,1,0:T(1,128)S(1)} all-gather(f32[1,1,2048]{2,1,0:T(1,128)S(1)} %bitcast.566), channel_id=1, replica_groups=mesh['chain'=8,'depth_0'=4,'depth_1'=8] {'depth_0'}, dimensions={0}, use_global_device_ids=true | all-gather | bytes 40960 | tf_op jit(solution)/shard_map/all_gather | solution.py:22
  123.3 8.6 %all-gather.14.cloned.1.call-done = f32[128,2048]{1,0:T(8,128)} async-done(((f32[16,2048]{1,0:T(8,128)}), f32[128,2048]{1,0:T(8,128)}) %all-gather.14.cloned.1.call-update) | async-done | bytes 1048592 | tf_op jit(solution)/shard_map/all_gather | solution.py:22
  131.9 1.4 fusion.22
  133.3 13.3 %all_gather.60 = f32[4,16,2048]{2,1,0:T(8,128)S(1)} all-gather(f32[1,16,2048]{2,1,0:T(8,128)S(1)} %get-tuple-element.309), channel_id=1, replica_groups=mesh['chain'=8,'depth_0'=4,'depth_1'=8] {'depth_0'}, dimensions={0}, use_global_device_ids=true | all-gather | bytes 655360 | tf_op jit(solution)/shard_map/all_gather | solution.py:22
  146.6 1.4 fusion.21
  149.0 5.7 %fusion.41 = f32[2,256]{1,0:T(2,128)S(1)} fusion(bf16[256,16384]{1,0:T(8,128)(2,1)} %bitcast.502, bf16[1,16384]{1,0:T(2,128)(2,1)S(1)} %bitcast.509, bf16[1,16384]{1,0:T(2,128)(2,1)S(1)} %bitcast.510), kind=kOutput, calls=%fused_computation.93 | convolution fusion | flops 16908288 | bytes 8456192 | tf_op jit(solution)/shard_map/dot_general | solution.py:102
  155.3 6.4 %all-to-all-start = ((f32[32,2,256]{2,1,0:T(2,128)}), f32[32,2,256]{2,1,0:T(2,128)S(1)}, u32[]{:S(2)}, u32[]{:S(2)}) async-start(f32[32,2,256]{2,1,0:T(2,128)} %broadcast_in_dim.38), calls=%async_computation | async-start | bytes 131072 | tf_op jit(solution)/shard_map/all_to_all | solution.py:34
  163.0 8.8 %all-to-all-done = f32[32,2,256]{2,1,0:T(2,128)S(1)} async-done(((f32[32,2,256]{2,1,0:T(2,128)}), f32[32,2,256]{2,1,0:T(2,128)S(1)}, u32[]{:S(2)}, u32[]{:S(2)}) %all-to-all-start) | async-done | bytes 65568 | tf_op jit(solution)/shard_map/all_to_all | solution.py:34
  172.4 3.8 %all-to-all-start.1 = ((f32[32,1,1]{2,1,0:T(1,128)}), f32[32,1,1]{2,1,0:T(1,128)S(1)}, u32[]{:S(2)}, u32[]{:S(2)}) async-start(f32[32,1,1]{2,1,0:T(1,128)} %broadcast_in_dim.39), calls=%async_computation.1 | async-start | bytes 32768 | tf_op jit(solution)/shard_map/all_to_all | solution.py:34
  176.4 12.2 %fusion.2 = f32[1,8,2048]{2,0,1:T(1,128)S(1)} fusion(bf16[256,1,1]{0,1,2:T(2,128)(2,1)S(1)} %reshape.544, bf16[32,8,8,2048]{3,2,1,0:T(8,128)(2,1)} %bitcast.504), kind=kOutput, calls=%fused_computation.14 | convolution fusion | flops 8388608 | bytes 8454656 | tf_op jit(solution)/shard_map/dot_general | solution.py:109
  189.3 25.7 %all-gather.6 = f32[8,1,2048]{2,1,0:T(1,128)S(1)} all-gather(f32[1,1,2048]{2,1,0:T(1,128)S(1)} %fusion.49), channel_id=1, replica_groups=mesh['chain'=8,'depth_0'=4,'depth_1'=8] {'depth_1'}, dimensions={0}, use_global_device_ids=true | all-gather | bytes 73728 | tf_op jit(solution)/shard_map/all_gather | solution.py:22
  215.2 10.5 %while.45 = (s32[]{:T(128)}, f32[16,2048]{1,0:T(8,128)S(1)}, f32[8,16,2048]{2,1,0:T(8,128)S(1)}, f32[8,2048]{1,0:T(8,128)S(1)}, s32[8]{0:T(128)S(1)}, /*index=5*...) while((s32[]{:T(128)}, f32[16,2048]{1,0:T(8,128)S(1)}, ...), condition=%wide.region_11.12_spmd.clone, body=%wide.region_10.11_spmd.clone.sunk | while | flops 131091 | bytes 549583 | solution.py:73
  227.2 12.3 %all-gather.7 = f32[4,1,2048]{2,1,0:T(1,128)S(1)} all-gather(f32[1,1,2048]{2,1,0:T(1,128)S(1)} %get-tuple-element.315), channel_id=1, replica_groups=mesh['chain'=8,'depth_0'=4,'depth_1'=8] {'depth_0'}, dimensions={0}, use_global_device_ids=true | all-gather | bytes 40960 | tf_op jit(solution)/shard_map/all_gather | solution.py:22
  239.6 25.4 %all-gather.16.cloned.1.call-done = f32[128,2048]{1,0:T(8,128)} async-done(((f32[16,2048]{1,0:T(8,128)}), f32[128,2048]{1,0:T(8,128)}) %all-gather.16.cloned.1.call-update) | async-done | bytes 1048592 | tf_op jit(solution)/shard_map/all_gather | solution.py:22
  265.1 1.4 fusion.10
  266.5 13.1 %all_gather.65 = f32[4,16,2048]{2,1,0:T(8,128)S(1)} all-gather(f32[1,16,2048]{2,1,0:T(8,128)S(1)} %get-tuple-element.300), channel_id=1, replica_groups=mesh['chain'=8,'depth_0'=4,'depth_1'=8] {'depth_0'}, dimensions={0}, use_global_device_ids=true | all-gather | bytes 655360 | tf_op jit(solution)/shard_map/all_gather | solution.py:22
  279.6 1.4 fusion.9
  283.2 6.4 %all-to-all-start.2 = ((f32[32,1,1]{2,1,0:T(1,128)}), f32[32,1,1]{2,1,0:T(1,128)S(1)}, u32[]{:S(2)}, u32[]{:S(2)}) async-start(f32[32,1,1]{2,1,0:T(1,128)} %broadcast_in_dim.40), calls=%async_computation.2 | async-start | bytes 32768 | tf_op jit(solution)/shard_map/all_to_all | solution.py:34
  290.2 9.2 %all-to-all-done.2 = f32[32,1,1]{2,1,0:T(1,128)S(1)} async-done(((f32[32,1,1]{2,1,0:T(1,128)}), f32[32,1,1]{2,1,0:T(1,128)S(1)}, u32[]{:S(2)}, u32[]{:S(2)}) %all-to-all-start.2) | async-done | bytes 160 | tf_op jit(solution)/shard_map/all_to_all | solution.py:34
  (198 shorter events, 40.5 us)
Async XLA Ops:
  7.2 83.9 %copy-start.4 = (f32[8,16,2048]{2,1,0:T(8,128)S(1)}, f32[8,16,2048]{2,1,0:T(8,128)}, u32[]{:S(2)}) copy-start(f32[8,16,2048]{2,1,0:T(8,128)} %param.18) | copy-start | bytes 3145732
  7.2 68.3 %all-gather.12.cloned.1.call-start = ((), (), s32[]{:S(2)}) async-start(), calls=%async_computation.3 | async-start | bytes 1179648 | tf_op jit(solution)/shard_map/all_gather | solution.py:22
  33.1 98.8 %all-gather.14.cloned.1.call-start = ((), (), s32[]{:S(2)}) async-start(), calls=%async_computation.4 | async-start | bytes 1179648 | tf_op jit(solution)/shard_map/all_gather | solution.py:22
  61.5 13.3 %copy-start.21 = (f32[1,2048]{1,0:T(1,128)}, f32[1,2048]{1,0:T(1,128)S(1)}, u32[]{:S(2)}) copy-start(f32[1,2048]{1,0:T(1,128)S(1)} %get-tuple-element.338) | copy-start | bytes 24580
  61.5 28.1 %copy-start.23 = (f32[1,2048]{1,0:T(1,128)}, f32[1,2048]{1,0:T(1,128)S(1)}, u32[]{:S(2)}) copy-start(f32[1,2048]{1,0:T(1,128)S(1)} %get-tuple-element.339) | copy-start | bytes 24580
  74.2 15.5 %copy-start.17 = (f32[1,2048]{1,0:T(1,128)}, f32[1,2048]{1,0:T(1,128)S(1)}, u32[]{:S(2)}) copy-start(f32[1,2048]{1,0:T(1,128)S(1)} %get-tuple-element.336) | copy-start | bytes 24580
  74.8 16.2 %copy-start.11 = (f32[1,2048]{1,0:T(1,128)}, f32[1,2048]{1,0:T(1,128)S(1)}, u32[]{:S(2)}) copy-start(f32[1,2048]{1,0:T(1,128)S(1)} %get-tuple-element.330) | copy-start | bytes 24580
  74.8 16.2 %copy-start.13 = (f32[1,2048]{1,0:T(1,128)}, f32[1,2048]{1,0:T(1,128)S(1)}, u32[]{:S(2)}) copy-start(f32[1,2048]{1,0:T(1,128)S(1)} %get-tuple-element.331) | copy-start | bytes 24580
  74.8 16.2 %copy-start.19 = (f32[1,2048]{1,0:T(1,128)}, f32[1,2048]{1,0:T(1,128)S(1)}, u32[]{:S(2)}) copy-start(f32[1,2048]{1,0:T(1,128)S(1)} %get-tuple-element.332) | copy-start | bytes 24580
  94.7 16.5 %copy-start.9 = (f32[8,2048]{1,0:T(8,128)S(1)}, f32[8,2048]{1,0:T(8,128)}, u32[]{:S(2)}) copy-start(f32[8,2048]{1,0:T(8,128)} %param.21) | copy-start | bytes 196612
  94.7 16.5 %copy-start.26 = (f32[1,2048]{1,0:T(1,128)S(1)}, f32[1,2048]{1,0:T(1,128)}, u32[]{:S(2)}) copy-start(f32[1,2048]{1,0:T(1,128)} %get-tuple-element.308) | copy-start | bytes 24580
  94.7 28.4 %copy-start.24 = (f32[1,2048]{1,0:T(1,128)S(1)}, f32[1,2048]{1,0:T(1,128)}, u32[]{:S(2)}) copy-start(f32[1,2048]{1,0:T(1,128)} %copy-done.23) | copy-start | bytes 24580
  94.7 28.5 %copy-start.5 = (f32[8,16,2048]{2,1,0:T(8,128)S(1)}, f32[8,16,2048]{2,1,0:T(8,128)}, u32[]{:S(2)}) copy-start(f32[8,16,2048]{2,1,0:T(8,128)} %get-tuple-element.306) | copy-start | bytes 3145732
  94.7 37.1 %copy-start.12 = (f32[1,2048]{1,0:T(1,128)S(1)}, f32[1,2048]{1,0:T(1,128)}, u32[]{:S(2)}) copy-start(f32[1,2048]{1,0:T(1,128)} %copy-done.11) | copy-start | bytes 24580
  94.7 37.1 %copy-start.14 = (f32[1,2048]{1,0:T(1,128)S(1)}, f32[1,2048]{1,0:T(1,128)}, u32[]{:S(2)}) copy-start(f32[1,2048]{1,0:T(1,128)} %copy-done.13) | copy-start | bytes 24580
  94.7 37.1 %copy-start.18 = (f32[1,2048]{1,0:T(1,128)S(1)}, f32[1,2048]{1,0:T(1,128)}, u32[]{:S(2)}) copy-start(f32[1,2048]{1,0:T(1,128)} %copy-done.17) | copy-start | bytes 24580
  94.8 37.1 %copy-start.20 = (f32[1,2048]{1,0:T(1,128)S(1)}, f32[1,2048]{1,0:T(1,128)}, u32[]{:S(2)}) copy-start(f32[1,2048]{1,0:T(1,128)} %copy-done.19) | copy-start | bytes 24580
  94.8 37.1 %copy-start.22 = (f32[1,2048]{1,0:T(1,128)S(1)}, f32[1,2048]{1,0:T(1,128)}, u32[]{:S(2)}) copy-start(f32[1,2048]{1,0:T(1,128)} %copy-done.21) | copy-start | bytes 24580
  94.8 51.8 %copy-start.25 = (f32[1,2048]{1,0:T(1,128)S(1)}, f32[1,2048]{1,0:T(1,128)}, u32[]{:S(2)}) copy-start(f32[1,2048]{1,0:T(1,128)} %get-tuple-element.307) | copy-start | bytes 24580
  94.8 53.2 %copy-start.7 = (f32[8,2048]{1,0:T(8,128)S(1)}, f32[8,2048]{1,0:T(8,128)}, u32[]{:S(2)}) copy-start(f32[8,2048]{1,0:T(8,128)} %get-tuple-element.326) | copy-start | bytes 196612
  94.8 53.5 %copy-start.6 = (f32[8,2048]{1,0:T(8,128)S(1)}, f32[8,2048]{1,0:T(8,128)}, u32[]{:S(2)}) copy-start(f32[8,2048]{1,0:T(8,128)} %param.14) | copy-start | bytes 196612
  94.8 53.5 %copy-start.16 = (f32[2048]{0:T(1024)S(1)}, f32[2048]{0:T(1024)}, u32[]{:S(2)}) copy-start(f32[2048]{0:T(1024)} %copy-done.15) | copy-start | bytes 24580
  123.2 53.1 %copy-start.27 = (f32[256]{0:T(256)S(1)}, f32[256]{0:T(256)}, u32[]{:S(2)}) copy-start(f32[256]{0:T(256)} %param.20) | copy-start | bytes 3076
  149.0 39.6 %copy-start.10 = (f32[8,2048]{1,0:T(8,128)S(1)}, f32[8,2048]{1,0:T(8,128)}, u32[]{:S(2)}) copy-start(f32[8,2048]{1,0:T(8,128)} %param.21) | copy-start | bytes 196612
  154.7 60.5 %copy-start.1 = (f32[16,2048]{1,0:T(8,128)S(1)}, f32[16,2048]{1,0:T(8,128)}, u32[]{:S(2)}) copy-start(f32[16,2048]{1,0:T(8,128)} %get-tuple-element.562) | copy-start | bytes 393220
  154.7 60.5 %copy-start.28 = (s32[16]{0:T(128)S(1)}, s32[16]{0:T(128)}, u32[]{:S(2)}) copy-start(s32[16]{0:T(128)} %get-tuple-element.574) | copy-start | bytes 196
  154.7 60.5 %copy-start.30 = (s32[8]{0:T(128)S(1)}, s32[8]{0:T(128)}, u32[]{:S(2)}) copy-start(s32[8]{0:T(128)} %copy-done.29) | copy-start | bytes 100
  155.3 16.4 %all-to-all-start = ((f32[32,2,256]{2,1,0:T(2,128)}), f32[32,2,256]{2,1,0:T(2,128)S(1)}, u32[]{:S(2)}, u32[]{:S(2)}) async-start(f32[32,2,256]{2,1,0:T(2,128)} %broadcast_in_dim.38), calls=%async_computation | async-start | bytes 131072 | tf_op jit(solution)/shard_map/all_to_all | solution.py:34
  172.4 110.1 %all-to-all-start.1 = ((f32[32,1,1]{2,1,0:T(1,128)}), f32[32,1,1]{2,1,0:T(1,128)S(1)}, u32[]{:S(2)}, u32[]{:S(2)}) async-start(f32[32,1,1]{2,1,0:T(1,128)} %broadcast_in_dim.39), calls=%async_computation.1 | async-start | bytes 32768 | tf_op jit(solution)/shard_map/all_to_all | solution.py:34
  176.3 88.8 %all-gather.16.cloned.1.call-start = ((), (), s32[]{:S(2)}) async-start(), calls=%async_computation.5 | async-start | bytes 1179648 | tf_op jit(solution)/shard_map/all_gather | solution.py:22
  189.2 112.1 %copy-start.8 = (f32[8,2048]{1,0:T(8,128)}, f32[8,2048]{1,0:T(8,128)S(1)}, u32[]{:S(2)}) copy-start(f32[8,2048]{1,0:T(8,128)S(1)} %get-tuple-element.297) | copy-start | bytes 196612
  283.2 16.2 %all-to-all-start.2 = ((f32[32,1,1]{2,1,0:T(1,128)}), f32[32,1,1]{2,1,0:T(1,128)S(1)}, u32[]{:S(2)}, u32[]{:S(2)}) async-start(f32[32,1,1]{2,1,0:T(1,128)} %broadcast_in_dim.40), calls=%async_computation.2 | async-start | bytes 32768 | tf_op jit(solution)/shard_map/all_to_all | solution.py:34
  (5 other events, 3.6 us)
Sparse Core Ops, SparseCore 0:
  33.2 41.2 all-gather.11
  94.8 37.0 all-gather.13
  226.6 38.4 all-gather.15
where the time goes:
time: 310 us; the launch traced here: 309 us
  blocking collectives  130 us (42%)
  waiting for transfers between devices  52.1 us (17%)
  other arithmetic  41.8 us (13%)
  local copies, waits for them, and re-layouts  30.5 us (10%)
  between operations  19.3 us (6%)
  matrix products  17.8 us (6%)
  starting transfers between devices  16.8 us (5%)
    all_gather x8, blocking collectives, prefix_by_axis(): pieces = jax.tree.map(lambda part: lax.all_gather(part, axis), subtotal)  130 us
    all_gather x3, waiting for transfers between devices, prefix_by_axis(): pieces = jax.tree.map(lambda part: lax.all_gather(part, axis), subtotal)  34 us
    unnamed x65, local copies, waits for them, and re-layouts  18.5 us
    all_to_all x3, waiting for transfers between devices, copy_for_each(): lax.all_to_all(jnp.broadcast_to(shard[None], (count, *shard.shape)), axis...  18 us
    all_to_all x3, starting transfers between devices, copy_for_each(): lax.all_to_all(jnp.broadcast_to(shard[None], (count, *shard.shape)), axis...  16.7 us
    eq x16, other arithmetic, advance(): source_depth == layer  15.1 us
    dot_general x1, matrix products, local(): jnp.dot(mixed, flat_basis, preferred_element_type=jnp.float32)  12.2 us
    dynamic_slice x40, local copies, waits for them, and re-layouts, march_down(): last, fields = lax.scan(advance, start, (decay, layers))  9.74 us
  transfers between devices with their start and end apart: 6, of which 4 were waited for; matrix products, arithmetic and copies ran while one was open for 15% of the time, Pallas kernels for 0%

commit v1 on v0

v1 whole, which is shorter than its diff:
```python
import jax
import jax.numpy as jnp
from jax import lax
from jax.sharding import Mesh
from jax.sharding import PartitionSpec as P

DEPTH = ("depth",)
LANES = 128


def decays(model, column_rate, depth_count):
    coef = (column_rate / depth_count)[None, :] * jnp.exp(0.5 * model)
    return coef, jnp.exp(-coef)


def slab_march(decay, wavelets, source_depth, first, observed):
    layers, sources = decay.shape[0], wavelets.shape[0]
    product, state = None, jnp.zeros_like(wavelets)
    products, own, taps, squares = [], [], jnp.zeros_like(wavelets), 0.0
    for z in range(layers):
        product = decay[z] if z == 0 else product * decay[z]
        state = decay[z][None] * state + jnp.where((source_depth == first + z)[:, None], wavelets, 0.0)
        products.append(product)
        own.append(state)
        taps = taps + product[None] * observed[z]
        squares = squares + product * product
    return products, own, taps, squares


def to_owners(rows, total, squares):
    blocks = rows.shape[1] // LANES
    q = rows.reshape(2, 8, blocks, LANES).transpose(2, 0, 1, 3).reshape(2 * blocks, 8, LANES)
    shared = jnp.stack([total, squares]).reshape(2, blocks, LANES).transpose(1, 0, 2)
    shared = jnp.repeat(shared, 2, axis=0)
    return jnp.concatenate([q, shared], axis=1)


def exchange(blocks):
    return lax.all_to_all(blocks, DEPTH, 0, 0, tiled=True)


def owner_carries(got, sd_half, layers):
    slabs = got.shape[0]
    carries = []
    carry = jnp.zeros_like(got[0, :8])
    for j in range(slabs):
        carries.append(carry)
        inside = jnp.logical_and(sd_half >= j * layers, sd_half < (j + 1) * layers)[:, None]
        carry = got[j, 8:9] * carry + jnp.where(inside, got[j, :8], 0.0)
    return carries


def local(model, column_rate, wavelets, source_depth, observed, basis, curvature, noise):
    layers, width = model.shape
    slabs = lax.axis_size(DEPTH)
    me = lax.axis_index(DEPTH)
    sources = wavelets.shape[0]
    first = me * layers
    above = (source_depth < first)[:, None]
    blocks = width // LANES
    half = me % 2
    sd_half = lax.dynamic_slice_in_dim(source_depth, half * 8, 8)

    coef, decay = decays(model, column_rate, slabs * layers)
    products, own, taps, squares = slab_march(decay, wavelets, source_depth, first, observed)
    got = exchange(to_owners(jnp.where(above, taps, own[-1]), products[-1], squares))
    carries = owner_carries(got, sd_half, layers)
    below = jnp.zeros_like(carries[0])
    back = [None] * slabs
    for i in reversed(range(slabs)):
        over = (sd_half < i * layers)[:, None]
        inside = jnp.logical_and(sd_half >= i * layers, sd_half < (i + 1) * layers)[:, None]
        sent = jnp.where(over, carries[i], jnp.where(inside, below, 0.0))
        rest = jnp.sum(jnp.where(over, below, 0.0), axis=0, keepdims=True)
        back[i] = jnp.concatenate([sent, rest], axis=0)
        below = below + carries[i] * (carries[i] * got[i, 9:10] - got[i, :8])
    mine = exchange(jnp.stack(back))
    sent = mine[:, :8].reshape(blocks, 2, 8, LANES).transpose(1, 2, 0, 3).reshape(sources, width)
    rest = mine[:, 8].reshape(blocks, 2, LANES).sum(1).reshape(width)
    carry = jnp.where(above, sent, 0.0)
    acc = jnp.where(above, 0.0, sent)
    rows, misfit = [None] * layers, 0.0
    for z in reversed(range(layers)):
        field = carry * products[z][None] + own[z]
        resid = field - observed[z]
        misfit = misfit + resid * resid
        acc = acc + field * resid
        rows[z] = rest + jnp.sum(jnp.where((source_depth < first + z)[:, None], acc, 0.0), axis=0)
    gradient = model - coef / sources * jnp.stack(rows)
    gain = jnp.sum(misfit) / sources + 0.5 * jnp.sum(model * model)

    f32 = jnp.float32
    p = jnp.sum(basis.astype(f32) * lax.reduce_precision(gradient, 8, 7)[None], axis=(1, 2))
    q = jnp.sum(basis.astype(f32) * lax.reduce_precision(noise, 8, 7)[None], axis=(1, 2))
    damping = curvature / (1.0 + curvature)
    shrink = 1.0 - 1.0 / jnp.sqrt(1.0 + curvature)
    part = damping * p - shrink * q
    mix = lax.reduce_precision(lax.all_gather(part, DEPTH).sum(0), 8, 7)
    correction = jnp.sum(mix[:, None, None] * basis.astype(f32), axis=0)
    proposal = model - gradient + noise + correction

    _, decay = decays(proposal, column_rate, slabs * layers)
    products, own, taps, squares = slab_march(decay, wavelets, source_depth, first, observed)
    got = exchange(to_owners(jnp.where(above, taps, own[-1]), products[-1], squares))
    misfit = 0.0
    for z in range(layers):
        resid = own[z] - observed[z]
        misfit = misfit + jnp.sum(resid * resid)
    carries = owner_carries(got, sd_half, layers)
    for j in range(slabs):
        misfit = misfit + jnp.sum(carries[j] * (carries[j] * got[j, 9:10] - 2.0 * got[j, :8]))
    gain = gain - (misfit / sources + 0.5 * jnp.sum(proposal * proposal))
    total = lax.all_gather(gain, DEPTH).sum(0)
    return proposal, jnp.reshape(total / (slabs * layers * width), (1,))


def solution(mesh):
    both = ("chain", "depth")
    in_specs = (
        P(both, None), P("chain"), P("chain", None), P("chain"), P(both, None, None),
        P("chain", "depth", None), P("chain"), P(both, None),
    )
    out_specs = (P(both, None), P("chain"))
    return jax.shard_map(local, mesh=mesh, in_specs=in_specs, out_specs=out_specs, check_vma=False)
```

time: 310 us -> 271 us (0.87)
  other arithmetic: 41.8 us -> 76.8 us
  waiting for transfers between devices: 52.1 us -> 22.2 us
  local copies, waits for them, and re-layouts: 30.5 us -> 3.28 us
  matrix products: 17.8 us -> 0 us
  blocking collectives: 130 us -> 115 us
  between operations: 19.3 us -> 29.8 us
  starting transfers between devices: 16.8 us -> 21.4 us
    all_gather x8 -> x1, blocking collectives: 130 us -> 41.4 us  [local(): mix = lax.reduce_precision(lax.all_gather(part, DEPTH).sum(0), 8, 7)]
    unnamed x0 -> x1, blocking collectives: none -> 73.6 us
    all_gather x3 -> x0, waiting for transfers between devices: 34 us -> none  [prefix_by_axis(): pieces = jax.tree.map(lambda part: lax.all_gather(part, axis), subtotal)]
    select_n x0 -> x32, other arithmetic: none -> 23.1 us  [local(): sent = jnp.where(over, carries[i], jnp.where(inside, below, 0.0))]
    reduce_sum x8 -> x25, other arithmetic: 5.69 us -> 27.3 us  [the longest x1 7.24 us: local(): jnp.sum(basis.astype(f32) * lax.reduce_precision(noise, 8, 7)[None], axis...]
    unnamed x7 -> x31, other arithmetic: 0.11 us -> 18.5 us
    dot_general x2 -> x0, matrix products: 17.8 us -> none  [the longest x1 12.2 us: local(): jnp.dot(mixed, flat_basis, preferred_element_type=jnp.float32)]
    unnamed x65 -> x17, local copies, waits for them, and re-layouts: 18.5 us -> 2.44 us
  transfers between devices with their start and end apart: 6 -> 3, of which waited for: 4 -> 3; matrix products, arithmetic and copies ran while one was open for 15% -> 2% of each run, Pallas kernels for 0% -> 0%
where the time goes in v1:
time: 271 us; the launch traced here: 269 us
  blocking collectives  115 us (42%)
  other arithmetic  76.8 us (28%)
  between operations  29.8 us (11%)
  waiting for transfers between devices  22.2 us (8%)
  starting transfers between devices  21.4 us (8%)
  local copies, waits for them, and re-layouts  3.28 us (1%)
    unnamed x1, blocking collectives  73.6 us
    all_gather x1, blocking collectives, local(): mix = lax.reduce_precision(lax.all_gather(part, DEPTH).sum(0), 8, 7)  41.4 us
    select_n x32, other arithmetic, local(): sent = jnp.where(over, carries[i], jnp.where(inside, below, 0.0))  23.1 us
    all_to_all x3, waiting for transfers between devices, exchange(): return lax.all_to_all(blocks, DEPTH, 0, 0, tiled=True)  22.2 us
    all_to_all x3, starting transfers between devices, exchange(): return lax.all_to_all(blocks, DEPTH, 0, 0, tiled=True)  21.4 us
    unnamed x31, other arithmetic  18.5 us
    reduce_sum x1, other arithmetic, local(): jnp.sum(basis.astype(f32) * lax.reduce_precision(noise, 8, 7)[None], axis...  7.24 us
    reduce_sum x8, other arithmetic, local(): jnp.sum(carries[j] * (carries[j] * got[j, 9:10] - 2.0 * got[j, :8]))  6.03 us
  transfers between devices with their start and end apart: 3, of which 3 were waited for; matrix products, arithmetic and copies ran while one was open for 2% of the time, Pallas kernels for 0%

profile of v1, /device:TPU:2, one launch (start us, length us, event | category | flops | bytes accessed | tf_op | source)
XLA Modules:
  0.0 268.5 jit_solution(945175610000464597)
XLA Ops:
  0.7 0.8 broadcast_multiply_fusion.2
  1.5 0.9 negate_exponential_fusion.1
  3.2 1.6 fusion.6
  5.6 11.5 %all-to-all-start = ((f32[32,10,128]{2,1,0:T(8,128)}), f32[32,10,128]{2,1,0:T(8,128)S(1)}, u32[]{:S(2)}, u32[]{:S(2)}) async-start(f32[32,10,128]{2,1,0:T(8,128)} %pad_maximum_fusion), calls=%async_computation | async-start | bytes 524288 | tf_op jit(solution)/shard_map/all_to_all | solution.py:39
  17.9 11.6 %all-to-all-done = f32[32,10,128]{2,1,0:T(8,128)S(1)} async-done(((f32[32,10,128]{2,1,0:T(8,128)}), f32[32,10,128]{2,1,0:T(8,128)S(1)}, u32[]{:S(2)}, u32[]{:S(2)}) %all-to-all-start) | async-done | bytes 163872 | tf_op jit(solution)/shard_map/all_to_all | solution.py:39
  35.5 0.8 select_select_fusion.8
  39.3 0.8 select_select_fusion.13
  42.4 0.8 select_select_fusion.17
  43.2 0.8 select_select_fusion.18
  43.9 0.8 select_select_fusion.19
  46.2 0.8 select_select_fusion.22
  49.3 0.8 select_select_fusion.26
  50.8 0.8 select_select_fusion.28
  51.5 0.8 select_select_fusion.29
  52.3 0.8 select_select_fusion.30
  72.3 4.4 %all-to-all-start.1 = ((f32[32,9,128]{2,1,0:T(8,128)}), f32[32,9,128]{2,1,0:T(8,128)S(1)}, u32[]{:S(2)}, u32[]{:S(2)}) async-start(f32[32,9,128]{2,1,0:T(8,128)} %constant_dynamic-update-slice_fusion), calls=%async_computation.1 | async-start | bytes 524288 | tf_op jit(solution)/shard_map/all_to_all | solution.py:39
  76.7 0.8 reduce_precision.14
  77.6 1.3 dynamic-slice
  78.9 9.4 %all-to-all-done.1 = f32[32,9,128]{2,1,0:T(8,128)S(1)} async-done(((f32[32,9,128]{2,1,0:T(8,128)}), f32[32,9,128]{2,1,0:T(8,128)S(1)}, u32[]{:S(2)}, u32[]{:S(2)}) %all-to-all-start.1) | async-done | bytes 147488 | tf_op jit(solution)/shard_map/all_to_all | solution.py:39
  88.4 1.2 select_reduce_fusion
  89.6 1.2 select_reduce_fusion.1
  90.8 1.2 select_reduce_fusion.2
  93.5 7.2 %fusion.1 = (f32[256]{0:T(256)S(1)}, f32[256]{0:T(256)S(1)}) fusion(bf16[256,8,2048]{2,1,0:T(8,128)(2,1)} %param.13, f32[8,2048]{1,0:T(8,128)S(1)} %reduce_precision.14, f32[8,2048]{1,0:T(8,128)S(1)} %get-tuple-element.325), kind=kLoop, calls=%fused_computation.4 | loop fusion | flops 20971008 | bytes 8521728 | tf_op jit(solution)/shard_map/reduce_sum | solution.py:94
  100.7 41.4 %all-gather.1 = f32[32,1,256]{2,1,0:T(1,128)S(1)} all-gather(f32[1,1,256]{2,1,0:T(1,128)S(1)} %bitcast.1342), channel_id=2, replica_groups=mesh['chain'=8,'depth'=32] {'depth'}, dimensions={0}, use_global_device_ids=true | all-gather | bytes 33792 | tf_op jit(solution)/shard_map/all_gather | solution.py:98
  142.2 5.1 %fusion.2 = f32[8,2048]{1,0:T(8,128)S(1)} fusion(bf16[256,8,2048]{2,1,0:T(8,128)(2,1)} %param.13, f32[256]{0:T(256)S(1)} %reduce_precision.15), kind=kLoop, calls=%fused_computation.5 | loop fusion | flops 12566528 | bytes 8455168 | tf_op jit(solution)/shard_map/reduce_sum | solution.py:99
  149.2 5.5 %all-to-all-start.2 = ((f32[32,10,128]{2,1,0:T(8,128)}), f32[32,10,128]{2,1,0:T(8,128)S(1)}, u32[]{:S(2)}, u32[]{:S(2)}) async-start(f32[32,10,128]{2,1,0:T(8,128)} %pad_maximum_fusion.1), calls=%async_computation.2 | async-start | bytes 524288 | tf_op jit(solution)/shard_map/all_to_all | solution.py:39
  154.7 0.9 add_reduce_fusion
  157.5 0.9 fusion.18
  162.2 0.8 fusion.8
  164.3 1.2 all-to-all-done.2
  170.1 0.8 multiply_reduce_fusion.5
  192.5 73.6 %all-reduce.1 = f32[32]{0:T(128)S(1)} all-reduce(f32[32]{0:T(128)S(1)} %dynamic-update-slice), channel_id=1, replica_groups=mesh['chain'=8,'depth'=32] {'depth'}, use_global_device_ids=true, to_apply=%add.1 | all-reduce | flops 32 | bytes 256
  (122 shorter events, 47.6 us)
Async XLA Ops:
  0.6 92.2 %copy-start.3 = (f32[8,2048]{1,0:T(8,128)S(1)}, f32[8,2048]{1,0:T(8,128)}, u32[]{:S(2)}) copy-start(f32[8,2048]{1,0:T(8,128)} %param.8) | copy-start | bytes 196612
  0.6 91.3 %copy-start = (f32[8,16,2048]{2,1,0:T(8,128)S(1)}, f32[8,16,2048]{2,1,0:T(8,128)}, u32[]{:S(2)}) copy-start(f32[8,16,2048]{2,1,0:T(8,128)} %param.12) | copy-start | bytes 3145732
  0.7 91.3 %copy-start.1 = (f32[16,2048]{1,0:T(8,128)S(1)}, f32[16,2048]{1,0:T(8,128)}, u32[]{:S(2)}) copy-start(f32[16,2048]{1,0:T(8,128)} %param.10) | copy-start | bytes 393220
  5.6 23.9 %all-to-all-start = ((f32[32,10,128]{2,1,0:T(8,128)}), f32[32,10,128]{2,1,0:T(8,128)S(1)}, u32[]{:S(2)}, u32[]{:S(2)}) async-start(f32[32,10,128]{2,1,0:T(8,128)} %pad_maximum_fusion), calls=%async_computation | async-start | bytes 524288 | tf_op jit(solution)/shard_map/all_to_all | solution.py:39
  29.5 0.7 copy-start.2
  29.6 71.1 %copy-start.6 = (f32[256]{0:T(256)S(1)}, f32[256]{0:T(256)}, u32[]{:S(2)}) copy-start(f32[256]{0:T(256)} %param.14) | copy-start | bytes 3076
  72.3 16.0 %all-to-all-start.1 = ((f32[32,9,128]{2,1,0:T(8,128)}), f32[32,9,128]{2,1,0:T(8,128)S(1)}, u32[]{:S(2)}, u32[]{:S(2)}) async-start(f32[32,9,128]{2,1,0:T(8,128)} %constant_dynamic-update-slice_fusion), calls=%async_computation.1 | async-start | bytes 524288 | tf_op jit(solution)/shard_map/all_to_all | solution.py:39
  93.5 53.8 %copy-start.4 = (f32[8,2048]{1,0:T(8,128)S(1)}, f32[8,2048]{1,0:T(8,128)}, u32[]{:S(2)}) copy-start(f32[8,2048]{1,0:T(8,128)} %param.15) | copy-start | bytes 196612
  147.9 119.5 %copy-start.5 = (f32[8,2048]{1,0:T(8,128)}, f32[8,2048]{1,0:T(8,128)S(1)}, u32[]{:S(2)}) copy-start(f32[8,2048]{1,0:T(8,128)S(1)} %get-tuple-element.62) | copy-start | bytes 196612
  149.2 16.3 %all-to-all-start.2 = ((f32[32,10,128]{2,1,0:T(8,128)}), f32[32,10,128]{2,1,0:T(8,128)S(1)}, u32[]{:S(2)}, u32[]{:S(2)}) async-start(f32[32,10,128]{2,1,0:T(8,128)} %pad_maximum_fusion.1), calls=%async_computation.2 | async-start | bytes 524288 | tf_op jit(solution)/shard_map/all_to_all | solution.py:39

commit v2 on v1

v2 whole, which is shorter than its diff:
```python
import functools

import jax
import jax.numpy as jnp
from jax import lax
from jax.experimental import pallas as pl
from jax.experimental.pallas import tpu as pltpu
from jax.sharding import PartitionSpec as P

LANES = 128
HALF = 8
F32 = jnp.float32


def columns(c):
    return pl.ds(pl.multiple_of(c * LANES, LANES), LANES)


def kernel(
    slabs, side, layers, sources, width, rank,
    sd_ref, model_hbm, rate_hbm, wave_hbm, obs_hbm, basis_hbm, curv_hbm, noise_hbm,
    prop_ref, gain_ref,
    model, rate, wave, obs, basis, curv, noise,
    sdv, coef, prods, own, wide, grad, rest, pbuf, mixcol, carries,
    out1, out1s, in1, in1s, out2, out2s, in2, in2s,
    out3, in3, out4, out4s, in4, in4s, out5, in5,
    load_sem, send_sem, recv_sem,
):
    me = lax.axis_index("depth")
    blocks = width // LANES
    first = me * layers
    rows = side
    cols = slabs // side
    pieces = 4
    per = rank // pieces

    loads = [
        pltpu.make_async_copy(src, dst, load_sem.at[i])
        for i, (src, dst) in enumerate(
            [(model_hbm, model), (rate_hbm, rate), (wave_hbm, wave), (obs_hbm, obs), (noise_hbm, noise), (curv_hbm, curv)]
        )
    ]
    basis_loads = [
        pltpu.make_async_copy(
            basis_hbm.at[pl.ds(i * per, per)], basis.at[pl.ds(i * per, per)], load_sem.at[len(loads) + i]
        )
        for i in range(pieces)
    ]
    for copy in loads + basis_loads:
        copy.start()

    def spread(size):
        steps = [size // 2]
        for n in range(1, size):
            steps.append((size // 2 - (n + 1) // 2) if n % 2 else (size // 2 + n // 2))
        return steps

    ys = [lax.rem(me // rows + dy, cols) * rows for dy in spread(cols)]
    zs = [lax.rem(lax.rem(me, rows) + dz, rows) for dz in spread(rows)]
    peers = [y + z for z in zs for y in ys][:-1]

    barrier = pltpu.get_barrier_semaphore()
    for other in peers:
        pl.semaphore_signal(barrier, inc=1, device_id={"depth": other}, device_id_type=pl.DeviceIdType.MESH)

    def send(step, other, pairs):
        for n, (block, landing) in enumerate(pairs):
            pltpu.make_async_remote_copy(
                src_ref=block(other),
                dst_ref=landing.at[me],
                send_sem=send_sem.at[step, n],
                recv_sem=recv_sem.at[step, n],
                device_id={"depth": other},
                device_id_type=pl.DeviceIdType.MESH,
            ).start()

    def send_all(step, pairs):
        for other in peers:
            send(step, other, pairs)

    def wait_all(sem, step, landings):
        for n, landing in enumerate(landings):
            part = landing.at[pl.ds(0, slabs - 1)]
            pltpu.make_async_copy(part, part, sem.at[step, n]).wait()

    for copy in loads[:4]:
        copy.wait()

    which = lax.broadcasted_iota(jnp.int32, (sources, LANES), 0)
    where_to = jnp.zeros((sources, LANES), jnp.int32)
    for k in range(sources):
        where_to = jnp.where(which == k, sd_ref[k], where_to)
    sdv[...] = where_to

    def march(c, field, main, shared, keep):
        at = columns(c)
        sd = sdv[...]
        above = sd < first
        factor = (rate[:, at] * (1.0 / (slabs * layers))) * jnp.exp(0.5 * field)
        decay = jnp.exp(-factor)
        if keep:
            coef[:, at] = factor
        source = wave[:, at]
        state = jnp.zeros((sources, LANES), F32)
        taps = jnp.zeros((sources, LANES), F32)
        misfit = jnp.zeros((sources, LANES), F32)
        product = squares = None
        for z in range(layers):
            d = decay[z : z + 1]
            product = d if z == 0 else product * d
            state = d * state + jnp.where(sd == first + z, source, 0.0)
            seen = obs[z, :, at]
            taps = taps + product * seen
            squares = product * product if z == 0 else squares + product * product
            if keep:
                prods[z : z + 1, at] = product
                own[z, :, at] = state
            else:
                miss = state - seen
                misfit = misfit + miss * miss
        block = jnp.where(above, taps, state)
        for h in range(sources // HALF):
            main[2 * c + h] = block[h * HALF : (h + 1) * HALF]
            shared[2 * c + h, 0:1] = product
            shared[2 * c + h, 1:2] = squares
        return misfit[:HALF] + misfit[HALF:]

    @pl.loop(0, blocks)
    def _(c):
        march(c, model[:, columns(c)], out1, out1s, True)

    in1[me] = out1[me]
    in1s[me] = out1s[me]
    pl.semaphore_wait(barrier, slabs - 1)
    send_all(0, [(lambda d: out1.at[d], in1), (lambda d: out1s.at[d], in1s)])

    for copy in loads[4:]:
        copy.wait()

    def project(values, first_time):
        parts = [values[:, c * LANES : (c + 1) * LANES] for c in range(blocks)]
        unroll = 8

        def some(i, _):
            for u in range(unroll):
                r = i * unroll + u
                vector = basis[r].astype(F32) if first_time else wide[r]
                if first_time:
                    wide[r] = vector
                total = vector[:, :LANES] * parts[0]
                for c in range(1, blocks):
                    total = total + vector[:, c * LANES : (c + 1) * LANES] * parts[c]
                pbuf[pl.ds(pl.multiple_of(r * layers, layers), layers), :] = total
            return 0

        for i in range(pieces if first_time else 1):
            if first_time:
                basis_loads[i].wait()
                lax.fori_loop(i * per // unroll, (i + 1) * per // unroll, some, 0)
            else:
                lax.fori_loop(0, rank // unroll, some, 0)
        folded = pbuf[pl.ds(0, rank, stride=layers), :]
        for s in range(1, layers):
            folded = folded + pbuf[pl.ds(s, rank, stride=layers), :]
        return lax.dot_general(
            jnp.ones((8, LANES), F32), folded, (((1,), (1,)), ((), ())),
            precision=lax.Precision.HIGHEST, preferred_element_type=F32,
        )[0:1]

    q = project(noise[...].astype(jnp.bfloat16).astype(F32), True)
    curvature = curv[...]
    damping = curvature / (1.0 + curvature)
    shrink = 1.0 - 1.0 / jnp.sqrt(1.0 + curvature)
    known = shrink * q

    sd_half = sdv[pl.ds(pl.multiple_of(lax.rem(me, 2) * HALF, HALF), HALF), :]
    group = 4

    def inside(j):
        return jnp.logical_and(sd_half >= j * layers, sd_half < (j + 1) * layers)

    wait_all(recv_sem, 0, [in1, in1s])

    def forward(i, carry):
        for u in range(group):
            j = i * group + u
            carries[j] = carry
            carry = in1s[j, 0:1] * carry + jnp.where(inside(j), in1[j], 0.0)
        return carry

    lax.fori_loop(0, slabs // group, forward, jnp.zeros((HALF, LANES), F32))

    def backward(i, below):
        for u in range(group):
            j = slabs - 1 - (i * group + u)
            over = sd_half < j * layers
            carry = carries[j]
            out2[j] = jnp.where(over, carry, jnp.where(inside(j), below, 0.0))
            out2s[j] = jnp.sum(jnp.where(over, below, 0.0), axis=0, keepdims=True)
            below = below + carry * (carry * in1s[j, 1:2] - in1[j])
        return below

    lax.fori_loop(0, slabs // group, backward, jnp.zeros((HALF, LANES), F32))
    in2[me] = out2[me]
    in2s[me] = out2s[me]
    send_all(1, [(lambda d: out2.at[d], in2), (lambda d: out2s.at[d], in2s)])
    wait_all(recv_sem, 1, [in2, in2s])

    layer_of = lax.broadcasted_iota(jnp.int32, (layers, LANES), 0)

    def slab(c, energy):
        at = columns(c)
        sd = sdv[...]
        above = sd < first
        sent = jnp.concatenate([in2[2 * c], in2[2 * c + 1]], axis=0)
        beyond = in2s[2 * c] + in2s[2 * c + 1]
        carry = jnp.where(above, sent, 0.0)
        acc = jnp.where(above, 0.0, sent)
        misfit = jnp.zeros((sources, LANES), F32)
        sums = jnp.zeros((layers, LANES), F32)
        for z in reversed(range(layers)):
            field = carry * prods[z : z + 1, at] + own[z, :, at]
            miss = field - obs[z, :, at]
            misfit = misfit + miss * miss
            acc = acc + field * miss
            held = jnp.where(sd < first + z, acc, 0.0)
            sums = jnp.where(
                layer_of == z, jnp.sum(held[:HALF] + held[HALF:], axis=0, keepdims=True), sums
            )
        old = model[:, at]
        g = old - coef[:, at] * (1.0 / sources) * (beyond + sums)
        grad[:, at] = g.astype(jnp.bfloat16).astype(F32)
        rest[:, at] = old - g + noise[:, at]
        return energy + (misfit[:HALF] + misfit[HALF:]) * (1.0 / sources) + 0.5 * (old * old)

    energy = lax.fori_loop(0, blocks, slab, jnp.zeros((HALF, LANES), F32))

    out3[...] = damping * project(grad[...], False) - known
    in3[me] = out3[...]
    send_all(2, [(lambda d: out3, in3)])
    wait_all(recv_sem, 2, [in3])
    total = in3[0]
    for j in range(1, slabs):
        total = total + in3[j]
    mix = total.astype(jnp.bfloat16).astype(F32)
    for h in range(rank // LANES):
        mixcol[h * LANES : (h + 1) * LANES] = jnp.broadcast_to(
            mix[:, h * LANES : (h + 1) * LANES], (LANES, LANES)
        ).T

    def correct(i, totals):
        unroll = 8
        for u in range(unroll):
            r = i * unroll + u
            weight = jnp.broadcast_to(mixcol[pl.ds(r, 1), :], (layers, LANES))
            vector = wide[r]
            totals = tuple(
                t + vector[:, c * LANES : (c + 1) * LANES] * weight for c, t in enumerate(totals)
            )
        return totals

    start = tuple(rest[:, c * LANES : (c + 1) * LANES] * 0.0 for c in range(blocks))
    correction = lax.fori_loop(0, rank // 8, correct, start)
    for c in range(blocks):
        at = slice(c * LANES, (c + 1) * LANES)
        prop_ref[:, at] = rest[:, at] + correction[c]

    energy_blocks = [(lambda d: out4.at[d], in4), (lambda d: out4s.at[d], in4s)]
    twos = [2 * lax.rem(lax.rem(me, rows) // 2 + dz, rows // 2) for dz in spread(rows // 2)]
    owners = [y + z for z in twos for y in ys]
    for n, owner in enumerate(owners):
        c = owner // 2
        new = prop_ref[:, columns(c)]
        energy = energy - march(c, new, out4, out4s, False) * (1.0 / sources) - 0.5 * (new * new)
        if n > 0:
            send(3, owners[n - 1], energy_blocks)
            send(3, owners[n - 1] + 1, energy_blocks)
    in4[me] = out4[me]
    in4s[me] = out4s[me]
    send(3, 2 * (me // 2) + 1 - lax.rem(me, 2), energy_blocks)
    wait_all(recv_sem, 3, [in4, in4s])

    def last(i, state):
        carry, energy = state
        for u in range(group):
            j = i * group + u
            block = in4[j]
            energy = energy - carry * (carry * in4s[j, 1:2] - 2.0 * block) * (1.0 / sources)
            carry = in4s[j, 0:1] * carry + jnp.where(inside(j), block, 0.0)
        return carry, energy

    _, energy = lax.fori_loop(0, slabs // group, last, (jnp.zeros((HALF, LANES), F32), energy))
    out5[...] = jnp.sum(energy, axis=0, keepdims=True)
    in5[me] = out5[...]
    send_all(4, [(lambda d: out5, in5)])
    wait_all(recv_sem, 4, [in5])
    total = in5[0]
    for j in range(1, slabs):
        total = total + in5[j]
    gain_ref[0] = jnp.sum(total) * (1.0 / (slabs * layers * width))
    for step, landings in enumerate([(in1, in1s), (in2, in2s), (in3,), (in4, in4s), (in5,)]):
        wait_all(send_sem, step, landings)


def hand_over(prop_ref, gain_ref, prop_out, gain_out):
    prop_out[...] = prop_ref[...]
    gain_out[0] = gain_ref[0]


def local(slabs, side, model, column_rate, wavelets, source_depth, observed, basis, curvature, noise):
    layers, width = model.shape
    sources, rank = wavelets.shape[0], basis.shape[0]
    anywhere = pl.BlockSpec(memory_space=pl.ANY)
    vmem = lambda *shape: pltpu.VMEM(shape, F32)
    exchange = lambda: [vmem(slabs, HALF, LANES), vmem(slabs, 2, LANES)] * 2
    prop, gain = pl.pallas_call(
        functools.partial(kernel, slabs, side, layers, sources, width, rank),
        out_shape=(
            jax.ShapeDtypeStruct((layers, width), F32),
            jax.ShapeDtypeStruct((1,), F32),
        ),
        in_specs=[pl.BlockSpec(memory_space=pltpu.SMEM)] + [anywhere] * 7,
        out_specs=(pl.BlockSpec(memory_space=pltpu.VMEM), pl.BlockSpec(memory_space=pltpu.SMEM)),
        scratch_shapes=[
            vmem(layers, width), vmem(1, width), vmem(sources, width), vmem(layers, sources, width),
            pltpu.VMEM((rank, layers, width), jnp.bfloat16), vmem(1, rank), vmem(layers, width),
            pltpu.VMEM((sources, LANES), jnp.int32), vmem(layers, width), vmem(layers, width),
            vmem(layers, sources, width), vmem(rank, layers, width), vmem(layers, width), vmem(layers, width),
            vmem(rank * layers, LANES), vmem(rank, LANES), vmem(slabs, HALF, LANES),
        ]
        + exchange()
        + [vmem(slabs, HALF, LANES), vmem(slabs, 1, LANES)] * 2
        + [vmem(1, rank), vmem(slabs, 1, rank)]
        + exchange()
        + [vmem(1, LANES), vmem(slabs, 1, LANES)]
        + [
            pltpu.SemaphoreType.DMA((10,)),
            pltpu.SemaphoreType.DMA((5, 2)),
            pltpu.SemaphoreType.DMA((5, 2)),
        ],
        compiler_params=pltpu.CompilerParams(
            collective_id=0, has_side_effects=True, vmem_limit_bytes=60 << 20
        ),
    )(
        source_depth, model, column_rate.reshape(1, width), wavelets, observed, basis,
        curvature.reshape(1, rank), noise,
    )
    whole = [pl.BlockSpec(memory_space=pltpu.VMEM), pl.BlockSpec(memory_space=pltpu.SMEM)]
    return pl.pallas_call(
        hand_over,
        out_shape=(jax.ShapeDtypeStruct((layers, width), F32), jax.ShapeDtypeStruct((1,), F32)),
        in_specs=whole,
        out_specs=tuple(whole),
    )(prop, gain)


def solution(mesh):
    both = ("chain", "depth")
    in_specs = (
        P(both, None), P("chain"), P("chain", None), P("chain"), P(both, None, None),
        P("chain", "depth", None), P("chain"), P(both, None),
    )
    out_specs = (P(both, None), P("chain"))
    body = functools.partial(local, mesh.shape["depth"], 8)
    return jax.shard_map(body, mesh=mesh, in_specs=in_specs, out_specs=out_specs, check_vma=False)
```

time: 271 us -> 48.3 us (0.18)
  blocking collectives: 115 us -> 0 us
  other arithmetic: 76.8 us -> 0 us
  Pallas kernels: 0 us -> 47.5 us
  between operations: 29.8 us -> 0.64 us
  waiting for transfers between devices: 22.2 us -> 0 us
  starting transfers between devices: 21.4 us -> 0 us
  local copies, waits for them, and re-layouts: 3.28 us -> 0 us
    unnamed x1 -> x0, blocking collectives: 73.6 us -> none
    pallas_call x0 -> x2, Pallas kernels: none -> 47.5 us  [the longest x1 45.4 us: local(): pl.pallas_call(functools.partial(kernel, slabs, side, layers, sources, wi...]
    all_gather x1 -> x0, blocking collectives: 41.4 us -> none  [local(): mix = lax.reduce_precision(lax.all_gather(part, DEPTH).sum(0), 8, 7)]
    reduce_sum x25 -> x0, other arithmetic: 27.3 us -> none  [the longest x1 7.24 us: local(): jnp.sum(basis.astype(f32) * lax.reduce_precision(noise, 8, 7)[None], axis...]
    select_n x32 -> x0, other arithmetic: 23.1 us -> none  [local(): sent = jnp.where(over, carries[i], jnp.where(inside, below, 0.0))]
    all_to_all x3 -> x0, waiting for transfers between devices: 22.2 us -> none  [exchange(): return lax.all_to_all(blocks, DEPTH, 0, 0, tiled=True)]
    all_to_all x3 -> x0, starting transfers between devices: 21.4 us -> none  [exchange(): return lax.all_to_all(blocks, DEPTH, 0, 0, tiled=True)]
    unnamed x31 -> x0, other arithmetic: 18.5 us -> none
  transfers between devices with their start and end apart: 3 -> 0, of which waited for: 3 -> 0; matrix products, arithmetic and copies ran while one was open for 2% -> 0% of each run, Pallas kernels for 0% -> 0%
where the time goes in v2:
time: 48.3 us; the launch traced here: 48.2 us
  Pallas kernels  47.5 us (98%)
  between operations  0.64 us (1%)
    pallas_call x1, Pallas kernels, local(): pl.pallas_call(functools.partial(kernel, slabs, side, layers, sources, wi...  45.4 us
    pallas_call x1, Pallas kernels, local(): pl.pallas_call(hand_over, out_shape=(jax.ShapeDtypeStruct((layers, width)...  2.1 us

profile of v2, /device:TPU:2, one launch (start us, length us, event | category | flops | bytes accessed | tf_op | source)
XLA Modules:
  0.0 48.2 jit_solution(17412678451131275578)
XLA Ops:
  0.6 45.4 %shard_map.95 = (f32[8,2048]{1,0:T(8,128)}, f32[1]{0:T(128)}) custom-call(s32[16]{0:T(128)} %sd_ref.1, f32[8,2048]{1,0:T(8,128)} %model_hbm.1, f32[1,2048]{1,0:T(1,128)} %bitcast.2, f32[16,2048]{1,0:T(8,128)} %wave_hbm.1, f32[8,16,2048]{2,1,0:T(8,128)} %obs_hbm.1, bf16[256,8,2048]{2,1,0:T(8,128)(2,1)} %basis_hbm.1, f32[1,256]{1,0:T(1,128)} %bitcast.3, ...), custom_call_target="tpu_custom_call" | custom-call | tf_op jit(solution)/shard_map/pallas_call | solution.py:316
  46.1 2.1 %shard_map.96 = (f32[8,2048]{1,0:T(8,128)}, f32[1]{0:T(128)}) custom-call(f32[8,2048]{1,0:T(8,128)} %get-tuple-element.4.prop_ref, f32[1]{0:T(128)} %get-tuple-element.5.gain_ref), custom_call_target="tpu_custom_call" | custom-call | tf_op jit(solution)/shard_map/pallas_call | solution.py:349

commit v3 on v2

--- a/solution.py
+++ b/solution.py
@@ -18,12 +18,11 @@
 
 def kernel(
     slabs, side, layers, sources, width, rank,
-    sd_ref, model_hbm, rate_hbm, wave_hbm, obs_hbm, basis_hbm, curv_hbm, noise_hbm,
+    sd_hbm, model_hbm, rate_hbm, wave_hbm, obs_hbm, basis_hbm, curv_hbm, noise_hbm,
     prop_ref, gain_ref,
-    model, rate, wave, obs, basis, curv, noise,
+    model, rate, wave, obs, basis, curv, noise, sd_ref,
     sdv, coef, prods, own, wide, grad, rest, pbuf, mixcol, carries,
-    out1, out1s, in1, in1s, out2, out2s, in2, in2s,
-    out3, in3, out4, out4s, in4, in4s, out5, in5,
+    out1, in1, out2, in2, out3, in3, out4, in4, out5, in5,
     load_sem, send_sem, recv_sem,
 ):
     me = lax.axis_index("depth")
@@ -37,7 +36,7 @@
     loads = [
         pltpu.make_async_copy(src, dst, load_sem.at[i])
         for i, (src, dst) in enumerate(
-            [(model_hbm, model), (rate_hbm, rate), (wave_hbm, wave), (obs_hbm, obs), (noise_hbm, noise), (curv_hbm, curv)]
+            [(model_hbm, model), (rate_hbm, rate), (wave_hbm, wave), (obs_hbm, obs), (noise_hbm, noise), (curv_hbm, curv), (sd_hbm, sd_ref)]
         )
     ]
     basis_loads = [
@@ -46,8 +45,6 @@
         )
         for i in range(pieces)
     ]
-    for copy in loads + basis_loads:
-        copy.start()
 
     def spread(size):
         steps = [size // 2]
@@ -62,6 +59,9 @@
     barrier = pltpu.get_barrier_semaphore()
     for other in peers:
         pl.semaphore_signal(barrier, inc=1, device_id={"depth": other}, device_id_type=pl.DeviceIdType.MESH)
+
+    for copy in loads + basis_loads:
+        copy.start()
 
     def send(step, other, pairs):
         for n, (block, landing) in enumerate(pairs):
@@ -83,7 +83,7 @@
             part = landing.at[pl.ds(0, slabs - 1)]
             pltpu.make_async_copy(part, part, sem.at[step, n]).wait()
 
-    for copy in loads[:4]:
+    for copy in loads[:4] + loads[6:]:
         copy.wait()
 
     which = lax.broadcasted_iota(jnp.int32, (sources, LANES), 0)
@@ -92,7 +92,7 @@
         where_to = jnp.where(which == k, sd_ref[k], where_to)
     sdv[...] = where_to
 
-    def march(c, field, main, shared, keep):
+    def march(c, field, main, keep):
         at = columns(c)
         sd = sdv[...]
         above = sd < first
@@ -120,21 +120,20 @@
                 misfit = misfit + miss * miss
         block = jnp.where(above, taps, state)
         for h in range(sources // HALF):
-            main[2 * c + h] = block[h * HALF : (h + 1) * HALF]
-            shared[2 * c + h, 0:1] = product
-            shared[2 * c + h, 1:2] = squares
+            main[2 * c + h, 0:HALF] = block[h * HALF : (h + 1) * HALF]
+            main[2 * c + h, HALF : HALF + 1] = product
+            main[2 * c + h, HALF + 1 : HALF + 2] = squares
         return misfit[:HALF] + misfit[HALF:]
 
     @pl.loop(0, blocks)
     def _(c):
-        march(c, model[:, columns(c)], out1, out1s, True)
+        march(c, model[:, columns(c)], out1, True)
 
     in1[me] = out1[me]
-    in1s[me] = out1s[me]
     pl.semaphore_wait(barrier, slabs - 1)
-    send_all(0, [(lambda d: out1.at[d], in1), (lambda d: out1s.at[d], in1s)])
-
-    for copy in loads[4:]:
+    send_all(0, [(lambda d: out1.at[d], in1)])
+
+    for copy in loads[4:6]:
         copy.wait()
 
     def project(values, first_time):
@@ -162,9 +161,13 @@
         folded = pbuf[pl.ds(0, rank, stride=layers), :]
         for s in range(1, layers):
             folded = folded + pbuf[pl.ds(s, rank, stride=layers), :]
+        high = folded.astype(jnp.bfloat16)
+        left = folded - high.astype(F32)
+        middle = left.astype(jnp.bfloat16)
+        low = (left - middle.astype(F32)).astype(jnp.bfloat16)
         return lax.dot_general(
-            jnp.ones((8, LANES), F32), folded, (((1,), (1,)), ((), ())),
-            precision=lax.Precision.HIGHEST, preferred_element_type=F32,
+            jnp.ones((8, 3 * LANES), jnp.bfloat16), jnp.concatenate([high, middle, low], axis=1),
+            (((1,), (1,)), ((), ())), preferred_element_type=F32,
         )[0:1]
 
     q = project(noise[...].astype(jnp.bfloat16).astype(F32), True)
@@ -179,13 +182,13 @@
     def inside(j):
         return jnp.logical_and(sd_half >= j * layers, sd_half < (j + 1) * layers)
 
-    wait_all(recv_sem, 0, [in1, in1s])
+    wait_all(recv_sem, 0, [in1])
 
     def forward(i, carry):
         for u in range(group):
             j = i * group + u
             carries[j] = carry
-            carry = in1s[j, 0:1] * carry + jnp.where(inside(j), in1[j], 0.0)
+            carry = in1[j, HALF : HALF + 1] * carry + jnp.where(inside(j), in1[j, 0:HALF], 0.0)
         return carry
 
     lax.fori_loop(0, slabs // group, forward, jnp.zeros((HALF, LANES), F32))
@@ -195,16 +198,15 @@
             j = slabs - 1 - (i * group + u)
             over = sd_half < j * layers
             carry = carries[j]
-            out2[j] = jnp.where(over, carry, jnp.where(inside(j), below, 0.0))
-            out2s[j] = jnp.sum(jnp.where(over, below, 0.0), axis=0, keepdims=True)
-            below = below + carry * (carry * in1s[j, 1:2] - in1[j])
+            out2[j, 0:HALF] = jnp.where(over, carry, jnp.where(inside(j), below, 0.0))
+            out2[j, HALF : HALF + 1] = jnp.sum(jnp.where(over, below, 0.0), axis=0, keepdims=True)
+            below = below + carry * (carry * in1[j, HALF + 1 : HALF + 2] - in1[j, 0:HALF])
         return below
 
     lax.fori_loop(0, slabs // group, backward, jnp.zeros((HALF, LANES), F32))
     in2[me] = out2[me]
-    in2s[me] = out2s[me]
-    send_all(1, [(lambda d: out2.at[d], in2), (lambda d: out2s.at[d], in2s)])
-    wait_all(recv_sem, 1, [in2, in2s])
+    send_all(1, [(lambda d: out2.at[d], in2)])
+    wait_all(recv_sem, 1, [in2])
 
     layer_of = lax.broadcasted_iota(jnp.int32, (layers, LANES), 0)
 
@@ -212,8 +214,8 @@
         at = columns(c)
         sd = sdv[...]
         above = sd < first
-        sent = jnp.concatenate([in2[2 * c], in2[2 * c + 1]], axis=0)
-        beyond = in2s[2 * c] + in2s[2 * c + 1]
+        sent = jnp.concatenate([in2[2 * c, 0:HALF], in2[2 * c + 1, 0:HALF]], axis=0)
+        beyond = in2[2 * c, HALF : HALF + 1] + in2[2 * c + 1, HALF : HALF + 1]
         carry = jnp.where(above, sent, 0.0)
         acc = jnp.where(above, 0.0, sent)
         misfit = jnp.zeros((sources, LANES), F32)
@@ -265,28 +267,27 @@
         at = slice(c * LANES, (c + 1) * LANES)
         prop_ref[:, at] = rest[:, at] + correction[c]
 
-    energy_blocks = [(lambda d: out4.at[d], in4), (lambda d: out4s.at[d], in4s)]
+    energy_blocks = [(lambda d: out4.at[d], in4)]
     twos = [2 * lax.rem(lax.rem(me, rows) // 2 + dz, rows // 2) for dz in spread(rows // 2)]
     owners = [y + z for z in twos for y in ys]
     for n, owner in enumerate(owners):
         c = owner // 2
         new = prop_ref[:, columns(c)]
-        energy = energy - march(c, new, out4, out4s, False) * (1.0 / sources) - 0.5 * (new * new)
+        energy = energy - march(c, new, out4, False) * (1.0 / sources) - 0.5 * (new * new)
         if n > 0:
             send(3, owners[n - 1], energy_blocks)
             send(3, owners[n - 1] + 1, energy_blocks)
     in4[me] = out4[me]
-    in4s[me] = out4s[me]
     send(3, 2 * (me // 2) + 1 - lax.rem(me, 2), energy_blocks)
-    wait_all(recv_sem, 3, [in4, in4s])
+    wait_all(recv_sem, 3, [in4])
 
     def last(i, state):
         carry, energy = state
         for u in range(group):
             j = i * group + u
-            block = in4[j]
-            energy = energy - carry * (carry * in4s[j, 1:2] - 2.0 * block) * (1.0 / sources)
-            carry = in4s[j, 0:1] * carry + jnp.where(inside(j), block, 0.0)
+            block = in4[j, 0:HALF]
+            energy = energy - carry * (carry * in4[j, HALF + 1 : HALF + 2] - 2.0 * block) * (1.0 / sources)
+            carry = in4[j, HALF : HALF + 1] * carry + jnp.where(inside(j), block, 0.0)
         return carry, energy
 
     _, energy = lax.fori_loop(0, slabs // group, last, (jnp.zeros((HALF, LANES), F32), energy))
@@ -297,14 +298,9 @@
     total = in5[0]
     for j in range(1, slabs):
         total = total + in5[j]
-    gain_ref[0] = jnp.sum(total) * (1.0 / (slabs * layers * width))
-    for step, landings in enumerate([(in1, in1s), (in2, in2s), (in3,), (in4, in4s), (in5,)]):
+    gain_ref[...] = total * (1.0 / (slabs * layers * width))
+    for step, landings in enumerate([(in1,), (in2,), (in3,), (in4,), (in5,)]):
         wait_all(send_sem, step, landings)
-
-
-def hand_over(prop_ref, gain_ref, prop_out, gain_out):
-    prop_out[...] = prop_ref[...]
-    gain_out[0] = gain_ref[0]
 
 
 def local(slabs, side, model, column_rate, wavelets, source_depth, observed, basis, curvature, noise):
@@ -312,29 +308,26 @@
     sources, rank = wavelets.shape[0], basis.shape[0]
     anywhere = pl.BlockSpec(memory_space=pl.ANY)
     vmem = lambda *shape: pltpu.VMEM(shape, F32)
-    exchange = lambda: [vmem(slabs, HALF, LANES), vmem(slabs, 2, LANES)] * 2
+    exchange = lambda rows: [vmem(slabs, HALF + rows, LANES)] * 2
     prop, gain = pl.pallas_call(
         functools.partial(kernel, slabs, side, layers, sources, width, rank),
-        out_shape=(
-            jax.ShapeDtypeStruct((layers, width), F32),
-            jax.ShapeDtypeStruct((1,), F32),
-        ),
-        in_specs=[pl.BlockSpec(memory_space=pltpu.SMEM)] + [anywhere] * 7,
-        out_specs=(pl.BlockSpec(memory_space=pltpu.VMEM), pl.BlockSpec(memory_space=pltpu.SMEM)),
+        out_shape=(pltpu.VMEM((layers, width), F32), pltpu.VMEM((1, LANES), F32)),
+        in_specs=[anywhere] * 8,
+        out_specs=(pl.BlockSpec(memory_space=pltpu.VMEM), pl.BlockSpec(memory_space=pltpu.VMEM)),
         scratch_shapes=[
             vmem(layers, width), vmem(1, width), vmem(sources, width), vmem(layers, sources, width),
             pltpu.VMEM((rank, layers, width), jnp.bfloat16), vmem(1, rank), vmem(layers, width),
-            pltpu.VMEM((sources, LANES), jnp.int32), vmem(layers, width), vmem(layers, width),
+            pltpu.SMEM((sources,), jnp.int32), pltpu.VMEM((sources, LANES), jnp.int32), vmem(layers, width), vmem(layers, width),
             vmem(layers, sources, width), vmem(rank, layers, width), vmem(layers, width), vmem(layers, width),
             vmem(rank * layers, LANES), vmem(rank, LANES), vmem(slabs, HALF, LANES),
         ]
-        + exchange()
-        + [vmem(slabs, HALF, LANES), vmem(slabs, 1, LANES)] * 2
+        + exchange(2)
+        + exchange(1)
         + [vmem(1, rank), vmem(slabs, 1, rank)]
-        + exchange()
+        + exchange(2)
         + [vmem(1, LANES), vmem(slabs, 1, LANES)]
         + [
-            pltpu.SemaphoreType.DMA((10,)),
+            pltpu.SemaphoreType.DMA((12,)),
             pltpu.SemaphoreType.DMA((5, 2)),
             pltpu.SemaphoreType.DMA((5, 2)),
         ],
@@ -345,13 +338,7 @@
         source_depth, model, column_rate.reshape(1, width), wavelets, observed, basis,
         curvature.reshape(1, rank), noise,
     )
-    whole = [pl.BlockSpec(memory_space=pltpu.VMEM), pl.BlockSpec(memory_space=pltpu.SMEM)]
-    return pl.pallas_call(
-        hand_over,
-        out_shape=(jax.ShapeDtypeStruct((layers, width), F32), jax.ShapeDtypeStruct((1,), F32)),
-        in_specs=whole,
-        out_specs=tuple(whole),
-    )(prop, gain)
+    return prop, jnp.sum(gain, axis=1)
 
 
 def solution(mesh):

time: 48.3 us -> 45.7 us (0.946)
  Pallas kernels: 47.5 us -> 43.8 us
  local copies, waits for them, and re-layouts: 0 us -> 0.63 us
  other arithmetic: 0 us -> 0.6 us
    pallas_call x1 -> x0, Pallas kernels: 2.1 us -> none  [local(): pl.pallas_call(hand_over, out_shape=(jax.ShapeDtypeStruct((layers, width)...]
    pallas_call x1, Pallas kernels: 45.4 us -> 43.8 us  [local(): pl.pallas_call(functools.partial(kernel, slabs, side, layers, sources, wi...]
    unnamed x0 -> x1, local copies, waits for them, and re-layouts: none -> 0.63 us
    reduce_sum x0 -> x1, other arithmetic: none -> 0.6 us  [local(): return (prop, jnp.sum(gain, axis=1))]
where the time goes in v3:
time: 45.7 us
  Pallas kernels  43.8 us (96%)
  between operations  0.64 us (1%)
  local copies, waits for them, and re-layouts  0.63 us (1%)
  other arithmetic  0.6 us (1%)
    pallas_call x1, Pallas kernels, local(): pl.pallas_call(functools.partial(kernel, slabs, side, layers, sources, wi...  43.8 us

profile of v3, /device:TPU:2, one launch (start us, length us, event | category | flops | bytes accessed | tf_op | source)
XLA Modules:
  0.0 45.7 jit_solution(14487485814442952357)
XLA Ops:
  0.6 43.8 %shard_map.95 = (f32[8,2048]{1,0:T(8,128)S(1)}, f32[1,128]{1,0:T(1,128)S(1)}) custom-call(s32[16]{0:T(128)} %sd_hbm.1, f32[8,2048]{1,0:T(8,128)} %model_hbm.1, f32[1,2048]{1,0:T(1,128)} %bitcast.3, f32[16,2048]{1,0:T(8,128)} %wave_hbm.1, f32[8,16,2048]{2,1,0:T(8,128)} %obs_hbm.1, bf16[256,8,2048]{2,1,0:T(8,128)(2,1)} %basis_hbm.1, f32[1,256]{1,0:T(1,128)} %bitcast.4, ...), custom_call_target="tpu_custom_call" | custom-call | tf_op jit(solution)/shard_map/pallas_call | solution.py:312
  44.4 0.6 %reduce_sum.11 = f32[]{:T(128)} reduce(f32[1,128]{1,0:T(1,128)S(1)} %get-tuple-element.5, f32[]{:T(128)} %constant.0.clone.1), dimensions={0,1}, to_apply=%region_0.0 | reduce | flops 127 | bytes 520 | tf_op jit(solution)/shard_map/reduce_sum | solution.py:341
  45.0 0.6 %copy.11 = f32[8,2048]{1,0:T(8,128)} copy(f32[8,2048]{1,0:T(8,128)S(1)} %get-tuple-element.6) | data formatting | bytes 131072
